TPU v7x, 32 devices: a whole 2x2x4 slice. The times are simulated.
32 devices in a mesh: frame: 16 (over z, y, core), head: 2 (over x).
Axes of the slice: x: 2, y: 2, z: 4, core: 2. Of those that a mesh axis runs over, the one named last changes fastest.
Arguments:
- tokens: bfloat16 [16384, 3072], P('frame'), may hold values from -6 to 6
- qkv_weight: bfloat16 [3, 3072, 3072], P(None, None, 'head'), may hold values from -0.109375 to 0.109375
- query_gain: float32 [128], replicated, may hold values from 0.1 to 1.9
- key_gain: float32 [128], replicated, may hold values from 0.1 to 1.9
- labels: int32 [24], P('head'), may hold values from 0 to 1, as said below
- space_mask: int32 [24, 16, 48], P('head'), may hold values from 0 to 1, as said below
- time_mask: int32 [24, 2, 2], P('head'), may hold values from 0 to 1, as said below
Outputs:
- attended: bfloat16 [16384, 3072], P(('frame', 'head'))
Inputs may be any that keep to these rules, and one draw needn't show every extreme that they name: `labels`: among heads 3 * j, 3 * j + 1 and 3 * j + 2 exactly one is temporal. space_mask[h, a, 16 + a] = 1 for every head and query block. For each head, at most 8 key blocks of the previous frame (b < 16) are allowed for some query block, and at most 8 of the next frame (b >= 32); some head reaches 8 on each side. time_mask[h, a, a] = 1 for every head and query block.
All inputs are finite; a program needn't handle non-finite values.
Results may differ from a plain program's by a relative error of at most 0.0073.
Values may be sent and summed in bfloat16 or wider, within the bound.
A program may use at most 192 MiB of HBM per device.

v0:
```python
import functools
import math

import jax
import jax.numpy as jnp
from jax import lax
from jax.experimental import pallas as pl
from jax.experimental.pallas import tpu as pltpu
from jax.sharding import PartitionSpec as P


STRIP = 8
BLOCK = 64
NEAR_MAX = 8
HD = 128
epsilon = 1e-06
BIG = 1e30
VMEM_LIMIT = 56 * 1024 * 1024


def chunk_rows(rows, want):
    while rows % want:
        want //= 2
    return want


def normed_head(projected, gains):
    inverse_rms = lax.rsqrt(jnp.mean(projected * projected, axis=-1, keepdims=True) + epsilon)
    return (projected * inverse_rms * gains).astype(jnp.bfloat16)


def project_kernel(kinds, pair, near_count, strips, table, x_ref, gq_ref, gk_ref, after_ref, *refs):
    weights = refs[: len(kinds) * pair]
    outs = refs[len(kinds) * pair :]
    out_ref = outs[0]
    i = pl.program_id(0)
    count = pl.num_programs(0) * pair
    step = x_ref.shape[0] // strips if strips > 1 else chunk_rows(x_ref.shape[0], 512)
    gains = {0: gq_ref[...], 1: gk_ref[...]}

    def body(m, carry):
        rows = pl.ds(pl.multiple_of(m * step, step), step)
        x = x_ref[rows, :]
        for n, kind in enumerate(kinds):
            w = [w_ref[...] for w_ref in weights[n * pair : (n + 1) * pair]]
            w = w[0] if pair == 1 else jnp.concatenate(w, axis=1)
            product = jnp.dot(x, w, preferred_element_type=jnp.float32)
            for j in range(pair):
                part = product[:, j * HD : (j + 1) * HD]
                if kind in gains:
                    part = normed_head(part, gains[kind])
                else:
                    part = part.astype(jnp.bfloat16)
                if strips:
                    pos = out_ref.shape[3]
                    if strips == 1:
                        per = step // pos
                        out_ref[pl.ds(m * per, per), n, j] = part.reshape(per, pos, HD)
                    else:
                        q = pos // strips
                        at = pl.ds(pl.multiple_of(m * q, q), q)
                        out_ref[:, n, j, at, :] = part.reshape(out_ref.shape[0], q, HD)
                else:
                    out_ref[n, j, rows, :] = part
        return carry

    lax.fori_loop(0, x_ref.shape[0] // step, body, 0)
    for j in range(pair if near_count else 0):
        head = i * pair + j
        for s in range(near_count):
            for side, ref in ((0, outs[1]), (1, outs[2])):
                b = table[count + (head * 2 + side) * near_count + s]
                src = pl.ds(pl.multiple_of(b * BLOCK, BLOCK), BLOCK)
                for n in range(2):
                    ref[n, j, s * BLOCK : (s + 1) * BLOCK, :] = out_ref[n, j, src, :]


def project(tokens, weight, gq, gk, heads, kinds, after, strips=0, deal=1, picks=None):
    rows, d = tokens.shape
    count = heads.shape[0]
    pair = 2 if count % 2 == 0 else 1
    n = len(kinds)
    near_count = 0 if picks is None else NEAR_MAX
    table = heads if picks is None else jnp.concatenate([heads, picks.reshape(-1)])

    def w_spec(kind, j):
        return pl.BlockSpec((None, d, HD), lambda i, t: (kind, 0, t[pair * i + j]))

    gain = pl.BlockSpec((1, HD), lambda i, t: (0, 0))
    if strips:
        pos = rows // strips
        shapes = [jax.ShapeDtypeStruct((strips, n, count, pos, HD), jnp.bfloat16)]
        specs = [pl.BlockSpec((strips, n, pair, pos, HD), lambda i, t: (0, 0, i, 0, 0))]
    else:
        shapes = [jax.ShapeDtypeStruct((n, count, rows, HD), jnp.bfloat16)]
        specs = [pl.BlockSpec((n, pair, rows, HD), lambda i, t: (0, i, 0, 0))]
    if near_count:
        near = near_count * BLOCK
        shapes += [jax.ShapeDtypeStruct((2, count, near, HD), jnp.bfloat16)] * 2
        specs += [pl.BlockSpec((2, pair, near, HD), lambda i, t: (0, i, 0, 0))] * 2
    out = pl.pallas_call(
        functools.partial(project_kernel, kinds, pair, near_count, deal if strips else 0),
        out_shape=tuple(shapes),
        grid_spec=pltpu.PrefetchScalarGridSpec(
            num_scalar_prefetch=1,
            grid=(count // pair,),
            in_specs=[
                pl.BlockSpec((rows, d), lambda i, t: (0, 0), pipeline_mode=pl.Buffered(1)),
                gain,
                gain,
                pl.BlockSpec(memory_space=pl.ANY),
            ]
            + [w_spec(kind, j) for kind in kinds for j in range(pair)],
            out_specs=tuple(specs),
        ),
        compiler_params=pltpu.CompilerParams(vmem_limit_bytes=VMEM_LIMIT),
        cost_estimate=pl.CostEstimate(
            flops=2 * rows * d * n * count * HD,
            bytes_accessed=2 * (rows * d + n * d * count * HD + n * rows * count * HD),
            transcendentals=0,
        ),
    )(table, tokens, gq, gk, after, *([weight] * (n * pair)))
    return out if near_count else out[0]


def attend_rows(queries, keys, values, factor):
    scores = lax.dot_general(
        queries, keys, (((1,), (1,)), ((), ())), preferred_element_type=jnp.float32
    )
    weight = jnp.exp2(scores * factor).astype(jnp.bfloat16)
    both = jnp.dot(weight, values, preferred_element_type=jnp.float32)
    return (both[:, :HD] / both[:, HD:]).astype(jnp.bfloat16)


def space_attend_kernel(factor, parts, side, q_ref, kv_ref, prev_ref, next_ref, bias_ref, after_ref, out_ref, ka, va, marks):
    rows = q_ref.shape[0]
    near = prev_ref.shape[1]
    total = rows + 2 * near

    @pl.when(pl.program_id(0) == 0)
    def _():
        va[:, HD:] = jnp.ones((total, HD), jnp.bfloat16)
        row = lax.broadcasted_iota(jnp.int32, (rows, HD), 0) // BLOCK
        lane = lax.broadcasted_iota(jnp.int32, (rows, HD), 1)
        marks[...] = jnp.where(row == lane, 1.0, 0.0).astype(jnp.bfloat16)

    for slot, ref in ((0, ka), (1, va)):
        ref[:rows, :HD] = kv_ref[slot]
        ref[rows : rows + near, :HD] = prev_ref[slot]
        ref[rows + near :, :HD] = next_ref[slot]
    for b in range(total // BLOCK):
        ka[b * BLOCK : (b + 1) * BLOCK, HD:] = jnp.broadcast_to(
            bias_ref[b : b + 1, :], (BLOCK, HD)
        ).astype(jnp.bfloat16)
    part = rows // parts
    step = chunk_rows(part, 256)
    for m in range(rows // step):
        span = slice(m * step, (m + 1) * step)
        queries = jnp.concatenate([q_ref[span, :], marks[span, :]], axis=1)
        result = attend_rows(queries, ka[...], va[...], factor)
        which = lax.rem(m * step // part - side[0] + parts, parts)
        first = m * step % part
        out_ref[which, first : first + step, :] = result


def space_attend(q, kv, prev_kv, next_kv, bias, parts, side, after):
    count = q.shape[1]
    rows = q.shape[2]
    near = prev_kv.shape[2]
    total = rows + 2 * near
    factor = math.log2(math.e) / math.sqrt(HD)
    near_spec = pl.BlockSpec((2, None, near, HD), lambda h, t: (0, h, 0, 0))
    part = rows // parts
    return pl.pallas_call(
        functools.partial(space_attend_kernel, factor, parts),
        out_shape=jax.ShapeDtypeStruct((parts, count, part, HD), jnp.bfloat16),
        grid_spec=pltpu.PrefetchScalarGridSpec(
            num_scalar_prefetch=1,
            grid=(count,),
            in_specs=[
                pl.BlockSpec((None, None, rows, HD), lambda h, t: (0, h, 0, 0)),
                pl.BlockSpec((2, None, rows, HD), lambda h, t: (0, h, 0, 0)),
                near_spec,
                near_spec,
                pl.BlockSpec((None, total // BLOCK, HD), lambda h, t: (h, 0, 0)),
                pl.BlockSpec(memory_space=pl.ANY),
            ],
            out_specs=pl.BlockSpec((parts, None, part, HD), lambda h, t: (0, h, 0, 0)),
            scratch_shapes=[
                pltpu.VMEM((total, 2 * HD), jnp.bfloat16),
                pltpu.VMEM((total, 2 * HD), jnp.bfloat16),
                pltpu.VMEM((rows, HD), jnp.bfloat16),
            ],
        ),
        compiler_params=pltpu.CompilerParams(vmem_limit_bytes=VMEM_LIMIT),
        cost_estimate=pl.CostEstimate(
            flops=8 * count * rows * total * HD,
            bytes_accessed=2 * HD * count * (4 * rows + 4 * near),
            transcendentals=count * rows * total,
        ),
        name="space_attend",
    )(side, q, kv, prev_kv, next_kv, bias, after)


def time_attend_kernel(factor, blocks, mask, x_ref, after_ref, out_ref, ka, va):
    frames, _, pos, _ = x_ref.shape
    rows = frames * pos
    span = pos * (BLOCK // STRIP)
    head = pl.program_id(0)
    ka[:, :HD] = x_ref[:, 1].reshape(rows, HD)
    va[:, :HD] = x_ref[:, 2].reshape(rows, HD)
    va[:, HD:] = jnp.ones((rows, HD), jnp.bfloat16)
    row = lax.broadcasted_iota(jnp.int32, (rows, HD), 0)
    lane = lax.broadcasted_iota(jnp.int32, (rows, HD), 1)
    strip = lax.rem(row, pos) // STRIP
    block = row // span
    lane_strip, lane_block = lane // blocks, lax.rem(lane, blocks)
    live = jnp.zeros((rows, HD), jnp.float32)
    for a in range(blocks):
        for b in range(blocks):
            m = mask[(head * blocks + a) * blocks + b].astype(jnp.float32)
            live = jnp.where((lane_block == a) & (block == b), m, live)
    live = jnp.where(strip == lane_strip, live, 0.0)
    ka[:, HD:] = ((live - 1.0) * BIG).astype(jnp.bfloat16)
    marks = jnp.where(strip * blocks + block == lane, 1.0, 0.0).astype(jnp.bfloat16)
    queries = jnp.concatenate([x_ref[:, 0].reshape(rows, HD), marks], axis=1)
    step = chunk_rows(rows, 256)
    per = step // pos
    parts, q = out_ref.shape[1], out_ref.shape[2]
    for m in range(rows // step):
        result = attend_rows(queries[m * step : (m + 1) * step], ka[...], va[...], factor)
        out_ref[m * per : (m + 1) * per] = result.reshape(per, parts, q, HD)


def time_attend(received, mask, after, deal):
    frames, _, count, pos, _ = received.shape
    rows = frames * pos
    factor = math.log2(math.e) / math.sqrt(HD)
    return pl.pallas_call(
        functools.partial(time_attend_kernel, factor, mask.shape[1]),
        out_shape=jax.ShapeDtypeStruct((frames, deal, count, pos // deal, HD), jnp.bfloat16),
        grid_spec=pltpu.PrefetchScalarGridSpec(
            num_scalar_prefetch=1,
            grid=(count,),
            in_specs=[
                pl.BlockSpec((frames, 3, None, pos, HD), lambda h, t: (0, 0, h, 0, 0)),
                pl.BlockSpec(memory_space=pl.ANY),
            ],
            out_specs=pl.BlockSpec((frames, deal, None, pos // deal, HD), lambda h, t: (0, 0, h, 0, 0)),
            scratch_shapes=[
                pltpu.VMEM((rows, 2 * HD), jnp.bfloat16),
                pltpu.VMEM((rows, 2 * HD), jnp.bfloat16),
            ],
        ),
        compiler_params=pltpu.CompilerParams(vmem_limit_bytes=VMEM_LIMIT),
        cost_estimate=pl.CostEstimate(
            flops=8 * count * rows * rows * HD,
            bytes_accessed=8 * HD * count * rows,
            transcendentals=count * rows * rows,
        ),
        name="time_attend",
    )(mask.reshape(-1), received, after)


def place_space_kernel(sources, table, *refs):
    h = pl.program_id(0)
    chosen = table[pl.num_programs(0) + h]
    out_ref = refs[-1]
    for n in range(sources):

        @pl.when(chosen == n)
        def _():
            out_ref[...] = refs[n][...]


def place_space(columns, chosen, sources, width):
    count = columns.shape[0]
    rows = sources[0][0].shape[1]

    def spec(n):
        return pl.BlockSpec((None, rows, HD), lambda h, t: (t[(2 + n) * count + h], 0, 0))

    return pl.pallas_call(
        functools.partial(place_space_kernel, len(sources)),
        out_shape=jax.ShapeDtypeStruct((rows, width), jnp.bfloat16),
        grid_spec=pltpu.PrefetchScalarGridSpec(
            num_scalar_prefetch=1,
            grid=(count,),
            in_specs=[spec(n) for n in range(len(sources))],
            out_specs=pl.BlockSpec((rows, HD), lambda h, t: (0, t[h])),
        ),
        cost_estimate=pl.CostEstimate(flops=0, bytes_accessed=4 * rows * count * HD, transcendentals=0),
        name="place_space",
    )(jnp.concatenate([columns, chosen] + [at for _, at in sources]), *[array for array, _ in sources])


def place_time_kernel(pick, count, table, timed_ref, placed_ref, out_ref, held, sems):
    copies = []
    for g in range(count):
        held[g] = pick(timed_ref, g).reshape(held.shape[1:])
        column = pl.ds(pl.multiple_of(table[g] * HD, HD), HD)
        copies.append(pltpu.make_async_copy(held.at[g], out_ref.at[:, column], sems.at[g]))
        copies[-1].start()
    for copy in copies:
        copy.wait()


def place_time(columns, timed, pick, placed):
    rows = placed.shape[0]
    count = columns.shape[0]
    return pl.pallas_call(
        functools.partial(place_time_kernel, pick, count),
        out_shape=jax.ShapeDtypeStruct(placed.shape, placed.dtype),
        grid_spec=pltpu.PrefetchScalarGridSpec(
            num_scalar_prefetch=1,
            grid=(1,),
            in_specs=[
                pl.BlockSpec(memory_space=pltpu.VMEM),
                pl.BlockSpec(memory_space=pl.ANY),
            ],
            out_specs=pl.BlockSpec(memory_space=pl.ANY),
            scratch_shapes=[
                pltpu.VMEM((count, rows, HD), jnp.bfloat16),
                pltpu.SemaphoreType.DMA((count,)),
            ],
        ),
        input_output_aliases={2: 0},
        compiler_params=pltpu.CompilerParams(vmem_limit_bytes=16 * 1024 * 1024),
        cost_estimate=pl.CostEstimate(
            flops=0, bytes_accessed=4 * rows * count * HD, transcendentals=0
        ),
        name="place_time",
    )(columns, timed, placed)


MESH = pl.DeviceIdType.MESH
FUSED_VMEM = 67_043_328


def spread(i, count):
    return count // 2 + ((i + 1) // 2) * (2 * lax.rem(i, 2) - 1)


def fused_kernel(
    factor,
    blocks,
    table,
    bias_ref,
    gq_ref,
    gk_ref,
    x_hbm,
    w_hbm,
    slots_hbm,
    own_hbm,
    other_hbm,
    back_hbm,
    their_hbm,
    x_v,
    w0k,
    w0v,
    w0q,
    w1k,
    w1v,
    w1q,
    tsend,
    trecv,
    kv,
    nsend,
    nrecv,
    qv,
    ka,
    va,
    marks,
    sout,
    tout,
    x_sem,
    w_sem,
    t_send,
    t_recv,
    n_send,
    n_recv,
    s_send,
    s_recv,
    o_sem,
    r_send,
    r_recv,
    l_send,
    l_recv,
):
    frames = lax.axis_size("frame")
    sides = lax.axis_size("head")
    me_f = lax.axis_index("frame")
    me_s = lax.axis_index("head")
    devices = frames * sides
    me = me_f * sides + me_s
    rows, _ = x_v.shape
    held = (((w0q, w0k, w0v), (w1q, w1k, w1v)))
    half = w0k.shape[0]
    groups = 2 * half
    pairs = groups // 2
    pos = tsend.shape[4]
    q = pos // sides
    slots_near = nsend.shape[4]
    near = slots_near * BLOCK
    total = ka.shape[0]
    step = rows // sides
    picks_at = 3 * groups
    mask_at = picks_at + groups * 2 * 2 * slots_near

    def x_copy(m):
        span = pl.ds(m * step, step)
        return pltpu.make_async_copy(x_hbm.at[span], x_v.at[span], x_sem.at[m])

    class Weights:
        def __init__(self, kind, g):
            self.parts = [
                pltpu.make_async_copy(
                    w_hbm.at[kind, :, pl.ds((3 * g + t) * HD, HD)], held[g // half][kind].at[g % half, t], w_sem.at[kind, g, t]
                )
                for t in range(3)
            ]

        def start(self):
            for copy in self.parts:
                copy.start()

        def wait(self):
            for copy in self.parts:
                copy.wait()

    w_copy = Weights

    order = [(kind, p * half + j) for p in range(2) for kind in (1, 2, 0) for j in range(half)]
    x_copy(0).start()
    for n, (kind, g) in enumerate(order):
        w_copy(kind, g).start()
        if n == 1:
            for m in range(1, sides):
                x_copy(m).start()

    barrier = pltpu.get_barrier_semaphore()

    def greet(i, c):
        other = lax.rem(me + i, devices)
        pl.semaphore_signal(
            barrier, inc=1, device_id={"frame": other // sides, "head": lax.rem(other, sides)}, device_id_type=MESH
        )
        return c

    lax.fori_loop(1, devices, greet, 0)

    row = lax.broadcasted_iota(jnp.int32, (rows, HD), 0)
    lane = lax.broadcasted_iota(jnp.int32, (rows, HD), 1)
    marks[...] = jnp.where(row // BLOCK == lane, 1.0, 0.0).astype(jnp.bfloat16)
    va[:, HD:] = jnp.ones((total, HD), jnp.bfloat16)
    gains = {0: gq_ref[...], 1: gk_ref[...]}

    @pl.when(me_f == 0)
    def _():
        nrecv[0] = jnp.zeros(nrecv.shape[1:], nrecv.dtype)

    @pl.when(me_f == frames - 1)
    def _():
        nrecv[1] = jnp.zeros(nrecv.shape[1:], nrecv.dtype)

    pl.semaphore_wait(barrier, devices - 1)
    labels_copy = pltpu.make_async_remote_copy(
        src_ref=slots_hbm,
        dst_ref=their_hbm,
        send_sem=l_send,
        recv_sem=l_recv,
        device_id={"frame": me_f, "head": 1 - me_s},
        device_id_type=MESH,
    )
    labels_copy.start()

    def time_slot(g):
        return table[g]

    def first_slot(g):
        return table[groups + g]

    def second_slot(g):
        return table[2 * groups + g]

    def weight(kind, p, g, slot):
        return held[p][kind][g - p * half, slot]

    def project_pair(kind, p, first, second, store, wait_x=False):
        def body(m, c):
            if wait_x:
                x_copy(m).wait()
            x = x_v[pl.ds(pl.multiple_of(m * step, step), step), :]
            w = jnp.concatenate([weight(kind, p, *first), weight(kind, p, *second)], axis=1)
            product = jnp.dot(x, w, preferred_element_type=jnp.float32)
            for j in range(2):
                part = product[:, j * HD : (j + 1) * HD]
                if kind in gains:
                    part = normed_head(part, gains[kind])
                else:
                    part = part.astype(jnp.bfloat16)
                store(m, j, part)
            return c

        lax.fori_loop(0, rows // step, body, 0)

    def time_project(p, wait_x):
        ga, gb = 2 * p, 2 * p + 1
        for n, kind in enumerate((1, 2, 0)):
            w_copy(kind, ga).wait()
            w_copy(kind, gb).wait()

            def store(m, j, part, kind=kind):
                at = pl.ds(pl.multiple_of(m * q, q), q)
                tsend[p, kind, :, j, at, :] = part.reshape(frames, q, HD)

            project_pair(kind, p, (ga, time_slot(ga)), (gb, time_slot(gb)), store, wait_x and n == 0)
            pltpu.make_async_copy(tsend.at[p, kind, me_f], trecv.at[p, kind, me_f], t_recv.at[p, kind]).start()

            def send(i, c, kind=kind):
                to = lax.rem(me_f + spread(i, frames), frames)
                pltpu.make_async_remote_copy(
                    src_ref=tsend.at[p, kind, to],
                    dst_ref=trecv.at[p, kind, me_f],
                    send_sem=t_send.at[p, kind],
                    recv_sem=t_recv.at[p, kind],
                    device_id={"frame": to, "head": me_s},
                    device_id_type=MESH,
                ).start()
                return c

            lax.fori_loop(0, frames - 1, send, 0)

    def near_copy(side, g):
        to = me_f + 1 if side == 0 else me_f - 1
        return pltpu.make_async_remote_copy(
            src_ref=nsend.at[side, g],
            dst_ref=nrecv.at[side, g],
            send_sem=n_send.at[side, g],
            recv_sem=n_recv.at[side, g],
            device_id={"frame": to, "head": me_s},
            device_id_type=MESH,
        )

    def space_project(p, g, c):
        for kind in (1, 2):

            def store(m, j, part, kind=kind):
                per = step // BLOCK
                kv[kind - 1, 2 * g + j, pl.ds(m * per, per)] = part.reshape(per, BLOCK, HD)

            project_pair(kind, p, (g, first_slot(g)), (g, second_slot(g)), store)
        for side in range(2):
            for j in range(2):
                for s in range(slots_near):
                    b = table[picks_at + ((2 * g + j) * 2 + side) * slots_near + s]
                    for n in range(2):
                        nsend[side, g, n, j, s] = kv[n, 2 * g + j, b]

        @pl.when(me_f < frames - 1)
        def _():
            near_copy(0, g).start()

        @pl.when(me_f > 0)
        def _():
            near_copy(1, g).start()

        return c

    def own_copy(g):
        span = pl.ds(2 * g, 2)
        return pltpu.make_async_copy(sout.at[0, span], own_hbm.at[span], o_sem.at[g])

    def other_copy(g):
        span = pl.ds(2 * g, 2)
        return pltpu.make_async_remote_copy(
            src_ref=sout.at[1, span],
            dst_ref=other_hbm.at[span],
            send_sem=s_send.at[g],
            recv_sem=s_recv.at[g],
            device_id={"frame": me_f, "head": 1 - me_s},
            device_id_type=MESH,
        )

    def space_mix(p, g, c):
        def store(m, j, part):
            qv[j, pl.ds(pl.multiple_of(m * step, step), step), :] = part

        project_pair(0, p, (g, first_slot(g)), (g, second_slot(g)), store)

        @pl.when(me_f > 0)
        def _():
            near_copy(0, g).wait_recv()

        @pl.when(me_f < frames - 1)
        def _():
            near_copy(1, g).wait_recv()

        def one(j, c):
            h = 2 * g + j
            for n, ref in ((0, ka), (1, va)):
                ref[:rows, :HD] = kv[n, h].reshape(rows, HD)
                ref[rows : rows + near, :HD] = nrecv[0, g, n, j].reshape(near, HD)
                ref[rows + near :, :HD] = nrecv[1, g, n, j].reshape(near, HD)
            for b in range(total // BLOCK):
                ka[b * BLOCK : (b + 1) * BLOCK, HD:] = jnp.broadcast_to(
                    bias_ref[h, b : b + 1, :], (BLOCK, HD)
                ).astype(jnp.bfloat16)
            part = rows // sides
            size = chunk_rows(part, 256)
            for m in range(rows // size):
                span = slice(m * size, (m + 1) * size)
                queries = jnp.concatenate([qv[j, span, :], marks[span, :]], axis=1)
                result = attend_rows(queries, ka[...], va[...], factor)
                which = lax.rem(m * size // part - me_s + sides, sides)
                first = m * size % part
                sout[which, h, first : first + size, :] = result
            return c

        lax.fori_loop(0, 2, one, 0)
        own_copy(g).start()
        other_copy(g).start()
        return c

    def time_mix(p):
        for kind in range(3):
            pltpu.make_async_copy(trecv.at[p, kind], trecv.at[p, kind], t_recv.at[p, kind]).wait()
        span = pos * (BLOCK // STRIP)

        def one(j, c):
            head = 2 * p + j
            ka[:rows, :HD] = trecv[p, 1, :, j].reshape(rows, HD)
            va[:rows, :HD] = trecv[p, 2, :, j].reshape(rows, HD)
            strip = lax.rem(row, pos) // STRIP
            block = row // span
            lane_strip, lane_block = lane // blocks, lax.rem(lane, blocks)
            live = jnp.zeros((rows, HD), jnp.float32)
            for a in range(blocks):
                for b in range(blocks):
                    m = table[mask_at + (head * blocks + a) * blocks + b].astype(jnp.float32)
                    live = jnp.where((lane_block == a) & (block == b), m, live)
            live = jnp.where(strip == lane_strip, live, 0.0)
            ka[:rows, HD:] = ((live - 1.0) * BIG).astype(jnp.bfloat16)
            tags = jnp.where(strip * blocks + block == lane, 1.0, 0.0).astype(jnp.bfloat16)
            queries = jnp.concatenate([trecv[p, 0, :, j].reshape(rows, HD), tags], axis=1)
            size = chunk_rows(rows, 256)
            per = size // pos
            for m in range(rows // size):
                result = attend_rows(queries[m * size : (m + 1) * size], ka[:rows], va[:rows], factor)
                tout[p, m * per * sides : (m + 1) * per * sides, j] = result.reshape(per * sides, q, HD)
            return c

        lax.fori_loop(0, 2, one, 0)
        heads = pl.ds(2 * p, 2)
        pltpu.make_async_copy(tout.at[p, me], back_hbm.at[me_f, me_s, heads], r_recv.at[p]).start()

        def send(i, c):
            to = lax.rem(me + spread(i, devices), devices)
            pltpu.make_async_remote_copy(
                src_ref=tout.at[p, to],
                dst_ref=back_hbm.at[me_f, me_s, heads],
                send_sem=r_send.at[p],
                recv_sem=r_recv.at[p],
                device_id={"frame": to // sides, "head": lax.rem(to, sides)},
                device_id_type=MESH,
            ).start()
            return c

        lax.fori_loop(0, devices - 1, send, 0)

    time_project(0, True)
    for p in range(1, pairs):
        time_project(p, False)
    for p in range(pairs):
        lax.fori_loop(2 * p, 2 * p + 2, functools.partial(space_project, p), 0)
    for p in range(pairs):
        lax.fori_loop(2 * p, 2 * p + 2, functools.partial(space_mix, p), 0)
        time_mix(p)

    def drain(g, c):
        own_copy(g).wait()
        other_copy(g).wait()

        @pl.when(me_f < frames - 1)
        def _():
            near_copy(0, g).wait_send()

        @pl.when(me_f > 0)
        def _():
            near_copy(1, g).wait_send()

        return c

    lax.fori_loop(0, groups, drain, 0)
    for p in range(pairs):
        for kind in range(3):
            sent = tsend.at[p, kind, pl.ds(0, frames - 1)]
            pltpu.make_async_copy(sent, sent, t_send.at[p, kind]).wait()
        sent = tout.at[p, pl.ds(0, devices - 1)]
        pltpu.make_async_copy(sent, sent, r_send.at[p]).wait()
        pltpu.make_async_copy(tout.at[p], tout.at[p], r_recv.at[p]).wait()
    labels_copy.wait()


def fused(tokens, weight, gq, gk, slots, first, second, picks, time_live, bias):
    rows, d = tokens.shape
    frames = lax.axis_size("frame")
    sides = lax.axis_size("head")
    groups = slots.shape[0]
    pairs = groups // 2
    heads = 2 * groups
    near = NEAR_MAX * BLOCK
    total = rows + 2 * near
    pos = rows // frames
    q = pos // sides
    part = rows // sides
    blocks = time_live.shape[1]
    table = jnp.concatenate([slots, first, second, picks.reshape(-1), time_live.reshape(-1)])
    slots_row = jnp.pad(slots, (0, HD - groups)).reshape(1, HD)
    bf = jnp.bfloat16
    any_spec = pl.BlockSpec(memory_space=pl.ANY)
    vmem_spec = pl.BlockSpec(memory_space=pltpu.VMEM)
    dma = pltpu.SemaphoreType.DMA
    return pl.pallas_call(
        functools.partial(fused_kernel, math.log2(math.e) / math.sqrt(HD), blocks),
        out_shape=(
            jax.ShapeDtypeStruct((heads, part, HD), bf),
            jax.ShapeDtypeStruct((heads, part, HD), bf),
            jax.ShapeDtypeStruct((frames, sides, groups, q, HD), bf),
            jax.ShapeDtypeStruct((1, HD), jnp.int32),
        ),
        in_specs=[pl.BlockSpec(memory_space=pltpu.SMEM), vmem_spec, vmem_spec, vmem_spec, any_spec, any_spec, any_spec],
        out_specs=(any_spec,) * 4,
        scratch_shapes=[
            pltpu.VMEM((rows, d), bf),
        ]
        + [pltpu.VMEM((groups // 2, 3, d, HD), bf)] * 6
        + [
            pltpu.VMEM((pairs, 3, frames, 2, pos, HD), bf),
            pltpu.VMEM((pairs, 3, frames, 2, pos, HD), bf),
            pltpu.VMEM((2, heads, rows // BLOCK, BLOCK, HD), bf),
            pltpu.VMEM((2, groups, 2, 2, NEAR_MAX, BLOCK, HD), bf),
            pltpu.VMEM((2, groups, 2, 2, NEAR_MAX, BLOCK, HD), bf),
            pltpu.VMEM((2, rows, HD), bf),
            pltpu.VMEM((total, 2 * HD), bf),
            pltpu.VMEM((total, 2 * HD), bf),
            pltpu.VMEM((rows, HD), bf),
            pltpu.VMEM((sides, heads, part, HD), bf),
            pltpu.VMEM((pairs, frames * sides, 2, q, HD), bf),
            dma((sides,)),
            dma((3, groups, 3)),
            dma((pairs, 3)),
            dma((pairs, 3)),
            dma((2, groups)),
            dma((2, groups)),
            dma((groups,)),
            dma((groups,)),
            dma((groups,)),
            dma((pairs,)),
            dma((pairs,)),
            dma,
            dma,
        ],
        compiler_params=pltpu.CompilerParams(
            vmem_limit_bytes=FUSED_VMEM, collective_id=0, has_side_effects=True
        ),
        name="fused",
    )(table, bias, gq, gk, tokens, weight, slots_row)


def place_kernel(mine_ref, theirs_ref, own_ref, other_ref, back_ref, out_ref):
    side = lax.axis_index("head")
    groups = back_ref.shape[2]
    rows = out_ref.shape[0]

    def put(head, value):
        out_ref[:, pl.ds(pl.multiple_of(head * HD, HD), HD)] = value

    for g in range(groups):
        for whose, slots, ref in ((side, mine_ref, own_ref), (1 - side, theirs_ref, other_ref)):
            slot = slots[0, g]
            base = 3 * (whose * groups + g)
            put(base + jnp.where(slot == 0, 1, 0), ref[2 * g])
            put(base + jnp.where(slot == 2, 1, 2), ref[2 * g + 1])
            put(base + slot, back_ref[:, whose, g].reshape(rows, HD))


def place(mine, theirs, own, other, back):
    heads, rows, _ = own.shape
    _, sides, groups, q, _ = back.shape
    size = chunk_rows(rows, 128)
    scalar = pl.BlockSpec(memory_space=pltpu.SMEM)
    space = pl.BlockSpec((heads, size, HD), lambda i: (0, i, 0))
    return pl.pallas_call(
        place_kernel,
        out_shape=jax.ShapeDtypeStruct((rows, sides * groups * 3 * HD), jnp.bfloat16),
        grid=(rows // size,),
        in_specs=[
            scalar,
            scalar,
            space,
            space,
            pl.BlockSpec((size // q, sides, groups, q, HD), lambda i: (i, 0, 0, 0, 0)),
        ],
        out_specs=pl.BlockSpec((size, sides * groups * 3 * HD), lambda i: (i, 0)),
        name="place",
    )(mine, theirs, own, other, back)


def block_picks(live):
    used = jnp.max(live, axis=1)
    width = used.shape[1]
    before = (jnp.arange(width)[:, None] < jnp.arange(width)[None, :]).astype(jnp.int32)
    rank = jnp.sum(used[:, :, None] * before[None], axis=1)
    return used[:, None, :] * (rank[:, None, :] == jnp.arange(NEAR_MAX)[None, :, None]).astype(jnp.int32)


def on_device(tokens, qkv_weight, query_gain, key_gain, labels, space_mask, time_mask):
    frame_count = lax.axis_size("frame")
    sides = lax.axis_size("head")
    own_frame = lax.axis_index("frame")
    own_side = lax.axis_index("head")
    row_count = tokens.shape[0]
    groups = labels.shape[0] // 3
    blocks = row_count // BLOCK
    space_count = 2 * groups
    gq, gk = query_gain.reshape(1, HD), key_gain.reshape(1, HD)

    picked = labels.reshape(groups, 3)
    time_slot = jnp.sum(picked * jnp.arange(3, dtype=jnp.int32)[None, :], axis=1)
    group_base = 3 * jnp.arange(groups, dtype=jnp.int32)
    time_heads = group_base + time_slot
    first_space = group_base + jnp.where(time_slot == 0, 1, 0)
    second_space = group_base + jnp.where(time_slot == 2, 1, 2)
    space_heads = jnp.stack([first_space, second_space], axis=1).reshape(space_count)

    live = jnp.take(space_mask, space_heads, axis=0)
    low, own, high = live[:, :, :blocks], live[:, :, blocks : 2 * blocks], live[:, :, 2 * blocks :]
    low_pick, high_pick = block_picks(low), block_picks(high)
    ids = jnp.arange(blocks, dtype=jnp.int32)
    picks = jnp.stack([jnp.sum(low_pick * ids, axis=-1), jnp.sum(high_pick * ids, axis=-1)], axis=1)
    low_ok = (own_frame > 0).astype(jnp.int32)
    high_ok = (own_frame < frame_count - 1).astype(jnp.int32)

    def near_live(pick, side, ok):
        return ok * jnp.sum(pick[:, :, None, :] * side[:, None, :, :], axis=-1)

    allowed = jnp.concatenate(
        [jnp.swapaxes(own, 1, 2), near_live(low_pick, low, low_ok), near_live(high_pick, high, high_ok)],
        axis=1,
    )
    bias = jnp.pad((allowed.astype(jnp.float32) - 1.0) * BIG, ((0, 0), (0, 0), (0, HD - blocks)))

    pos_count = row_count // frame_count
    deal = sides if pos_count % (sides * STRIP) == 0 else 1
    if sides == 2 and deal == 2 and groups == 4:
        mask = jnp.take(time_mask, time_heads, axis=0)
        own_out, other_out, back, theirs = fused(
            tokens, qkv_weight, gq, gk, time_slot, first_space - group_base, second_space - group_base, picks, mask, bias
        )
        mine = jnp.pad(time_slot, (0, HD - groups)).reshape(1, HD)
        return place(mine, theirs, own_out, other_out, back)
    up = [(i, i + 1) for i in range(frame_count - 1)]
    down = [(i + 1, i) for i in range(frame_count - 1)]
    swap = [(0, 1), (1, 0)]
    kv, to_next, to_prev = project(tokens, qkv_weight, gq, gk, space_heads, (1, 2), gq, picks=picks)
    prev_kv = lax.ppermute(to_next, "frame", up)
    next_kv = lax.ppermute(to_prev, "frame", down)
    packed = project(
        tokens, qkv_weight, gq, gk, time_heads, (0, 1, 2), kv, strips=frame_count, deal=deal
    )
    received = lax.all_to_all(packed, "frame", split_axis=0, concat_axis=0, tiled=True)
    query_heads = space_heads
    if sides == 2:
        their_slot = lax.ppermute(time_slot, "head", swap)
        query_heads, their_slot = lax.optimization_barrier((space_heads, their_slot))
        slots = jnp.where(
            own_side == 0,
            jnp.concatenate([time_slot, their_slot]),
            jnp.concatenate([their_slot, time_slot]),
        )
    else:
        slots = lax.all_to_all(
            jnp.broadcast_to(time_slot[None], (sides, groups)), "head", 0, 0, tiled=True
        ).reshape(-1)
    space_q = project(tokens, qkv_weight, gq, gk, query_heads, (0,), packed)

    side = jnp.reshape(own_side if sides == 2 else jnp.int32(0), (1,)).astype(jnp.int32)
    space_out = space_attend(space_q, kv, prev_kv, next_kv, bias, sides, side, space_q)
    mask = jnp.take(time_mask, time_heads, axis=0)
    time_out = time_attend(received, mask, space_out, deal)

    part_rows = row_count // sides
    total_heads = sides * space_count
    head_ids = jnp.arange(total_heads, dtype=jnp.int32)
    if sides == 2:
        space_recv = lax.ppermute(space_out[1], "head", swap)

        def clamped(whose):
            return jnp.clip(head_ids - whose * space_count, 0, space_count - 1)

        sources = [(space_out[0], clamped(own_side)), (space_recv, clamped(1 - own_side))]
        chosen = (head_ids // space_count != own_side).astype(jnp.int32)
    else:
        space_all = lax.all_to_all(space_out, "head", 0, 0, tiled=True)
        sources = [(space_all.reshape(total_heads, part_rows, HD), head_ids)]
        chosen = jnp.zeros_like(head_ids)
    all_groups = jnp.arange(sides * groups, dtype=jnp.int32)
    firsts = 3 * all_groups + jnp.where(slots == 0, 1, 0)
    seconds = 3 * all_groups + jnp.where(slots == 2, 1, 2)
    space_columns = jnp.stack([firsts, seconds], axis=1).reshape(total_heads)
    placed = place_space(space_columns, chosen, sources, sides * groups * 3 * HD)

    if deal == sides:
        q = pos_count // sides
        timed = lax.all_to_all(
            time_out.reshape(frame_count * sides, groups, q, HD), ("frame", "head"), 0, 0, tiled=True
        )
        timed = timed.reshape(frame_count, sides, groups, q, HD)

        def pick(ref, g):
            return ref[:, g // groups, g % groups]

    else:
        timed = time_out.reshape(frame_count, groups, pos_count, HD)
        timed = lax.all_to_all(timed, "frame", 0, 0, tiled=True)
        timed = lax.all_to_all(timed, "head", 0, 0, tiled=True)
        timed = timed.reshape(sides, frame_count // sides, groups, pos_count, HD)

        def pick(ref, g):
            return ref[g // groups, :, g % groups]

    return place_time(3 * all_groups + slots, timed, pick, placed)


def solution(mesh):
    placed = (
        P("frame", None),
        P(None, None, "head"),
        P(),
        P(),
        P("head"),
        P("head", None, None),
        P("head", None, None),
    )

    return jax.shard_map(
        on_device, mesh=mesh, in_specs=placed, out_specs=P(("frame", "head"), None), check_vma=False
    )
```

profile of v0, /device:TPU:0, one launch (start us, length us, event | category | flops | bytes accessed | tf_op | source)
XLA Modules:
  0.0 156.9 jit_solution(15839454669988809069)
XLA Ops:
  0.0 0.7 reshape.146
  0.7 0.1 multiply_reduce_fusion.6
  0.9 0.5 pad_bitcast_fusion.slots_hbm.mine_ref
  1.4 0.1 copy.21
  1.5 0.1 reshape.149
  1.6 0.1 reshape.148
  1.7 0.8 copy.25
  2.5 0.6 gather_fusion.1
  3.1 0.1 broadcast_select_fusion.1
  3.2 0.1 select_n.79
  3.3 1.4 gather_fusion
  4.7 0.1 copy.23
  4.8 0.1 broadcast_select_fusion
  4.9 0.3 slice_reduce_fusion.1
  5.3 0.1 multiply_reduce_fusion.3
  5.4 0.3 fusion.2
  5.8 0.1 reshape.150
  5.9 0.7 concatenate.6.table
  6.5 0.1 copy.26
  6.6 1.2 multiply_reduce_fusion.1
  7.8 0.1 copy.27
  7.9 1.2 multiply_reduce_fusion
  9.1 0.7 pad.10.bias_ref
  9.7 142.7 %fused.1 = (bf16[8,512,128]{2,1,0:T(8,128)(2,1)}, bf16[8,512,128]{2,1,0:T(8,128)(2,1)}, bf16[16,2,4,32,128]{4,3,2,1,0:T(8,128)(2,1)}, s32[1,128]{1,0:T(1,128)}) custom-call(s32[156]{0:T(256)} %concatenate.6.table, f32[8,32,128]{2,1,0:T(8,128)} %pad.10.bias_ref, f32[1,128]{1,0:T(1,128)} %bitcast.20, f32[1,128]{1,0:T(1,128)} %bitcast.21, ...), custom_call_target="tpu_custom_call" | custom-call | tf_op jit(solution)/shard_map/fused/pallas_call | solution.py:724
  152.4 4.5 %place.1 = bf16[512,3072]{1,0:T(8,128)(2,1)} custom-call(s32[1,128]{1,0:T(1,128)} %pad_bitcast_fusion.slots_hbm.mine_ref, s32[1,128]{1,0:T(1,128)} %get-tuple-element.9.theirs_ref, bf16[8,512,128]{2,1,0:T(8,128)(2,1)} %get-tuple-element.10.own_ref, bf16[8,512,128]{2,1,0:T(8,128)(2,1)} %get-tuple-element.11.other_ref, ...), custom_call_target="tpu_custom_call" | custom-call | tf_op jit(solution)/shard_map/place/pallas_call | solution.py:794
  (14 shorter events, 0.1 us)
where the time goes:
time: 157 us
  Pallas kernels  147 us (94%)
  local copies, waits for them, and re-layouts  6.09 us (4%)
  other arithmetic  3.5 us (2%)
    pallas_call x1, Pallas kernels, fused(): pl.pallas_call(functools.partial(fused_kernel, math.log2(math.e) / math.s...  143 us
    pallas_call x1, Pallas kernels, place(): pl.pallas_call(place_kernel, out_shape=jax.ShapeDtypeStruct((rows, sides...  4.49 us

commit v1 on v0

--- a/solution.py
+++ b/solution.py
@@ -345,6 +345,7 @@
     factor,
     blocks,
     table,
+    picks_ref,
     bias_ref,
     gq_ref,
     gk_ref,
@@ -404,8 +405,8 @@
     near = slots_near * BLOCK
     total = ka.shape[0]
     step = rows // sides
-    picks_at = 3 * groups
-    mask_at = picks_at + groups * 2 * 2 * slots_near
+    mask_at = 3 * groups
+    own_blocks = rows // BLOCK
 
     def x_copy(m):
         span = pl.ds(m * step, step)
@@ -553,7 +554,7 @@
         for side in range(2):
             for j in range(2):
                 for s in range(slots_near):
-                    b = table[picks_at + ((2 * g + j) * 2 + side) * slots_near + s]
+                    b = picks_ref[2 * g + j, own_blocks + side * slots_near + s]
                     for n in range(2):
                         nsend[side, g, n, j, s] = kv[n, 2 * g + j, b]
 
@@ -702,24 +703,22 @@
     labels_copy.wait()
 
 
-def fused(tokens, weight, gq, gk, slots, first, second, picks, time_live, bias):
+def fused(tokens, weight, gq, gk, table, slots_row, picks, bias, blocks):
     rows, d = tokens.shape
     frames = lax.axis_size("frame")
     sides = lax.axis_size("head")
-    groups = slots.shape[0]
+    heads = bias.shape[0]
+    groups = heads // 2
     pairs = groups // 2
-    heads = 2 * groups
     near = NEAR_MAX * BLOCK
     total = rows + 2 * near
     pos = rows // frames
     q = pos // sides
     part = rows // sides
-    blocks = time_live.shape[1]
-    table = jnp.concatenate([slots, first, second, picks.reshape(-1), time_live.reshape(-1)])
-    slots_row = jnp.pad(slots, (0, HD - groups)).reshape(1, HD)
     bf = jnp.bfloat16
     any_spec = pl.BlockSpec(memory_space=pl.ANY)
     vmem_spec = pl.BlockSpec(memory_space=pltpu.VMEM)
+    smem_spec = pl.BlockSpec(memory_space=pltpu.SMEM)
     dma = pltpu.SemaphoreType.DMA
     return pl.pallas_call(
         functools.partial(fused_kernel, math.log2(math.e) / math.sqrt(HD), blocks),
@@ -729,7 +728,7 @@
             jax.ShapeDtypeStruct((frames, sides, groups, q, HD), bf),
             jax.ShapeDtypeStruct((1, HD), jnp.int32),
         ),
-        in_specs=[pl.BlockSpec(memory_space=pltpu.SMEM), vmem_spec, vmem_spec, vmem_spec, any_spec, any_spec, any_spec],
+        in_specs=[smem_spec, smem_spec, vmem_spec, vmem_spec, vmem_spec, any_spec, any_spec, any_spec],
         out_specs=(any_spec,) * 4,
         scratch_shapes=[
             pltpu.VMEM((rows, d), bf),
@@ -765,7 +764,86 @@
             vmem_limit_bytes=FUSED_VMEM, collective_id=0, has_side_effects=True
         ),
         name="fused",
-    )(table, bias, gq, gk, tokens, weight, slots_row)
+    )(table, picks, bias, gq, gk, tokens, weight, slots_row)
+
+
+def tables_kernel(tblocks, labels_ref, time_ref, mask_ref, scalars_ref, slots_ref, picks_ref, bias_ref):
+    frames = lax.axis_size("frame")
+    me_f = lax.axis_index("frame")
+    count, blocks, wide = mask_ref.shape
+    groups = count // 3
+    near = NEAR_MAX
+    keys = blocks + 2 * near
+    low_ok = (me_f > 0).astype(jnp.float32)
+    high_ok = (me_f < frames - 1).astype(jnp.float32)
+    row = lax.broadcasted_iota(jnp.int32, (keys, wide), 0)
+    lane = lax.broadcasted_iota(jnp.int32, (keys, wide), 1)
+    side = jnp.where(row < blocks + near, 0, 1)
+    want = jnp.where(row < blocks, -1, row - blocks - side * near).astype(jnp.float32)
+    own = jnp.where(lane - blocks == row, 1.0, 0.0) * jnp.where(row < blocks, 1.0, 0.0)
+    ok = jnp.where(row < blocks, 1.0, jnp.where(side == 0, low_ok, high_ok))[:, :1]
+    inside = jnp.where(lane // blocks == side * 2, 1.0, 0.0)
+    before = lax.broadcasted_iota(jnp.int32, (wide, wide), 0)
+    after = lax.broadcasted_iota(jnp.int32, (wide, wide), 1)
+    earlier = jnp.where((before < after) & (before // blocks == after // blocks), 1.0, 0.0).astype(jnp.bfloat16)
+    name = lax.rem(lane, blocks).astype(jnp.float32)
+    bias_ref[...] = jnp.zeros(bias_ref.shape, bias_ref.dtype)
+    picks_ref[...] = jnp.zeros(picks_ref.shape, picks_ref.dtype)
+    for g in range(groups):
+        slot = labels_ref[3 * g + 1] + 2 * labels_ref[3 * g + 2]
+        first = jnp.where(slot == 0, 1, 0)
+        second = jnp.where(slot == 2, 1, 2)
+        scalars_ref[g] = slot
+        scalars_ref[groups + g] = first
+        scalars_ref[2 * groups + g] = second
+        slots_ref[0, g] = slot
+        for a in range(tblocks):
+            for b in range(tblocks):
+                at = 3 * groups + (g * tblocks + a) * tblocks + b
+                scalars_ref[at] = time_ref[((3 * g + slot) * tblocks + a) * tblocks + b]
+        for j, which in ((0, first), (1, second)):
+            live = mask_ref[3 * g + which].astype(jnp.float32)
+            used = jnp.max(live, axis=0, keepdims=True)
+            used = jnp.broadcast_to(used, (8, wide))
+            rank = jnp.dot(used.astype(jnp.bfloat16), earlier, preferred_element_type=jnp.float32)
+            chosen = jnp.where(rank[:1] == want, 1.0, 0.0) * used[:1] * inside
+            select = own + chosen
+            allowed = lax.dot_general(
+                select.astype(jnp.bfloat16),
+                live.astype(jnp.bfloat16),
+                (((1,), (1,)), ((), ())),
+                preferred_element_type=jnp.float32,
+            )
+            h = 2 * g + j
+            bias_ref[h, :, :blocks] = (allowed * ok - 1.0) * BIG
+            number = lax.dot_general(
+                name[:8].astype(jnp.bfloat16),
+                chosen.astype(jnp.bfloat16),
+                (((1,), (1,)), ((), ())),
+                preferred_element_type=jnp.float32,
+            )
+            picks_ref[h : h + 1, :keys] = number[:1].astype(jnp.int32)
+
+
+def tables(labels, time_mask, space_mask):
+    groups = labels.shape[0] // 3
+    blocks = space_mask.shape[1]
+    tblocks = time_mask.shape[1]
+    keys = blocks + 2 * NEAR_MAX
+    smem = pl.BlockSpec(memory_space=pltpu.SMEM)
+    vmem = pl.BlockSpec(memory_space=pltpu.VMEM)
+    return pl.pallas_call(
+        functools.partial(tables_kernel, tblocks),
+        out_shape=(
+            jax.ShapeDtypeStruct((groups * (3 + tblocks * tblocks),), jnp.int32),
+            jax.ShapeDtypeStruct((1, HD), jnp.int32),
+            jax.ShapeDtypeStruct((2 * groups, HD), jnp.int32),
+            jax.ShapeDtypeStruct((2 * groups, keys, HD), jnp.float32),
+        ),
+        in_specs=[smem, smem, vmem],
+        out_specs=(smem, smem, vmem, vmem),
+        name="tables",
+    )(labels, time_mask.reshape(-1), space_mask)
 
 
 def place_kernel(mine_ref, theirs_ref, own_ref, other_ref, back_ref, out_ref):
@@ -826,6 +904,15 @@
     space_count = 2 * groups
     gq, gk = query_gain.reshape(1, HD), key_gain.reshape(1, HD)
 
+    pos_count = row_count // frame_count
+    deal = sides if pos_count % (sides * STRIP) == 0 else 1
+    if sides == 2 and deal == 2 and groups == 4:
+        table, mine, picks, bias = tables(labels, time_mask, space_mask)
+        own_out, other_out, back, theirs = fused(
+            tokens, qkv_weight, gq, gk, table, mine, picks, bias, time_mask.shape[1]
+        )
+        return place(mine, theirs, own_out, other_out, back)
+
     picked = labels.reshape(groups, 3)
     time_slot = jnp.sum(picked * jnp.arange(3, dtype=jnp.int32)[None, :], axis=1)
     group_base = 3 * jnp.arange(groups, dtype=jnp.int32)
@@ -851,15 +938,6 @@
     )
     bias = jnp.pad((allowed.astype(jnp.float32) - 1.0) * BIG, ((0, 0), (0, 0), (0, HD - blocks)))
 
-    pos_count = row_count // frame_count
-    deal = sides if pos_count % (sides * STRIP) == 0 else 1
-    if sides == 2 and deal == 2 and groups == 4:
-        mask = jnp.take(time_mask, time_heads, axis=0)
-        own_out, other_out, back, theirs = fused(
-            tokens, qkv_weight, gq, gk, time_slot, first_space - group_base, second_space - group_base, picks, mask, bias
-        )
-        mine = jnp.pad(time_slot, (0, HD - groups)).reshape(1, HD)
-        return place(mine, theirs, own_out, other_out, back)
     up = [(i, i + 1) for i in range(frame_count - 1)]
     down = [(i + 1, i) for i in range(frame_count - 1)]
     swap = [(0, 1), (1, 0)]

time: 157 us -> 151 us (0.962)
  local copies, waits for them, and re-layouts: 6.09 us -> 1.42 us
  other arithmetic: 3.5 us -> 0 us
  Pallas kernels: 147 us -> 150 us
    pallas_call x0 -> x1, Pallas kernels: none -> 2.59 us  [tables(): pl.pallas_call(functools.partial(tables_kernel, tblocks), out_shape=(jax....]
    reduce_sum x4 -> x0, other arithmetic: 2.55 us -> none  [the longest x2 2.32 us: near_live(): return ok * jnp.sum(pick[:, :, None, :] * side[:, None, :, :], axis=-1)]
    gather x3 -> x0, local copies, waits for them, and re-layouts: 2.12 us -> none  [the longest x2 1.55 us: on_device(): live = jnp.take(space_mask, space_heads, axis=0)]
where the time goes in v1:
time: 151 us
  Pallas kernels  150 us (99%)
    pallas_call x1, Pallas kernels, fused(): pl.pallas_call(functools.partial(fused_kernel, math.log2(math.e) / math.s...  143 us
    pallas_call x1, Pallas kernels, place(): pl.pallas_call(place_kernel, out_shape=jax.ShapeDtypeStruct((rows, sides...  4.49 us

profile of v1, /device:TPU:0, one launch (start us, length us, event | category | flops | bytes accessed | tf_op | source)
XLA Modules:
  0.0 151.2 jit_solution(1059001898394660083)
XLA Ops:
  0.0 0.8 copy.9
  0.8 0.6 reshape.9.time_ref
  1.4 2.6 %tables.1 = (s32[28]{0:T(128)}, s32[1,128]{1,0:T(1,128)}, s32[8,128]{1,0:T(8,128)}, f32[8,32,128]{2,1,0:T(8,128)}) custom-call(s32[12]{0:T(128)} %labels_ref.1, s32[48]{0:T(128)} %reshape.9.time_ref, s32[12,16,48]{2,1,0:T(8,128)} %mask_ref.1), custom_call_target="tpu_custom_call" | custom-call | tf_op jit(solution)/shard_map/tables/pallas_call | solution.py:835
  4.0 142.7 %fused.1 = (bf16[8,512,128]{2,1,0:T(8,128)(2,1)}, bf16[8,512,128]{2,1,0:T(8,128)(2,1)}, bf16[16,2,4,32,128]{4,3,2,1,0:T(8,128)(2,1)}, s32[1,128]{1,0:T(1,128)}) custom-call(s32[28]{0:T(128)} %get-tuple-element.14.table, s32[8,128]{1,0:T(8,128)} %get-tuple-element.15.picks_ref, f32[8,32,128]{2,1,0:T(8,128)} %get-tuple-element.16.bias_ref, f32[1,128]{1,0:T(1,128)} %bitcast.2, ...), custom_call_target="tpu_custom_call" | custom-call | tf_op jit(solution)/shard_map/fused/pallas_call | solution.py:723
  146.7 4.5 %place.1 = bf16[512,3072]{1,0:T(8,128)(2,1)} custom-call(s32[1,128]{1,0:T(1,128)} %get-tuple-element.13.slots_hbm.mine_ref, s32[1,128]{1,0:T(1,128)} %get-tuple-element.17.theirs_ref, bf16[8,512,128]{2,1,0:T(8,128)(2,1)} %get-tuple-element.18.own_ref, bf16[8,512,128]{2,1,0:T(8,128)(2,1)} %get-tuple-element.19.other_ref, ...), custom_call_target="tpu_custom_call" | custom-call | tf_op jit(solution)/shard_map/place/pallas_call | solution.py:872
